TPU v7x, 128 devices: a whole 4x4x4 slice. The times are simulated.
128 devices in a mesh: corpus: 32 (over y, z, core), query: 4 (over x).
Axes of the slice: x: 4, y: 4, z: 4, core: 2. Of those that a mesh axis runs over, the one named last changes fastest.
Arguments:
- queries: bfloat16 [32768, 768], P(('corpus', 'query')), may hold values from -8 to 8
- probes: int32 [32768, 4], P(('corpus', 'query')), may hold values from 0 to 1023, as said below
- targets: int32 [32768, 8], P(('corpus', 'query')), may hold values from 0 to 4095, all different within a row
- passage_codes: int32 [1024, 96, 1024], P('corpus'), may hold values from 0 to 15
- codebook: float32 [16, 768], replicated, may hold values from -6 to 6
Outputs:
- grad_queries: bfloat16 [32768, 768], P(('corpus', 'query'))
- codebook_step: float32 [16, 768], replicated
Inputs may be any that keep to these rules, and one draw needn't show every extreme that they name: `probes`: each row names 4 different lists; list l belongs to index l // 32 of corpus. In every aligned block of 256 rows (the rows of one device) no list is named more than 2 times, and one list, the same one in every block, is named exactly 2 times. `targets`: each row names 8 different candidates; column r holds the candidate of rank r.
All inputs are finite; a program needn't handle non-finite values.
Results may differ from a plain program's by a relative error of at most 0.01.
The roundings to bfloat16 on the way count: a program that leaves them out, or rounds other values in their place, can miss the bound.
Values may be sent and summed in bfloat16 or wider, within the bound.
No kernel may reach another device: no remote copies, remote signals or barrier semaphores. Data moves between devices by JAX's collectives and lax.ppermute only.
A program may use at most 192 MiB of HBM per device.

v0:
```python
import jax
import jax.numpy as jnp
from jax import lax
from jax.sharding import PartitionSpec as P

D = 768
SUBSPACES = 96
CENTROIDS = 16
SUBDIM = 8
PASSAGES = 1024
PROBES = 4
TARGETS = 8
NEGATIVE = -1e30
EPSILON = 1e-06


def rank_weights():
    levels = jnp.arange(TARGETS, dtype=jnp.int32).astype(jnp.float32)
    return 2.0 * (TARGETS - levels) / (TARGETS * (TARGETS + 1.0))


def rank_slots(list_keys, key_count, keep):
    key_ids = jnp.arange(key_count, dtype=jnp.int32)
    marked = ((list_keys[:, None] == key_ids[None, :]) & keep[:, None]).astype(jnp.int32)
    running = jnp.cumsum(marked, axis=0)
    return jnp.sum(marked * running, axis=1) - 1


def note_block(probes, targets):
    row_count = probes.shape[0]
    probe_cols = jnp.arange(PROBES, dtype=jnp.int32)
    inside = targets[:, None, :] // PASSAGES == probe_cols[None, :, None]
    target_spot = jnp.where(inside, targets[:, None, :] % PASSAGES, -1)
    query_ids = jnp.broadcast_to(
        jnp.arange(row_count, dtype=jnp.int32)[:, None, None], (row_count, PROBES, 1)
    )
    return jnp.concatenate([query_ids, target_spot], axis=2).reshape(
        row_count * PROBES, TARGETS + 1
    )


def lookup_rows(rows_block, codebook):
    lead_shape = rows_block.shape[:-1]
    split_rows = rows_block.astype(jnp.float32).reshape(lead_shape + (SUBSPACES, SUBDIM))
    centroids = codebook.reshape(CENTROIDS, SUBSPACES, SUBDIM)
    lut_rows = jnp.einsum(
        "...me,kme->...mk", split_rows, centroids, precision=lax.Precision.HIGHEST
    )
    return lut_rows.reshape(lead_shape + (SUBSPACES * CENTROIDS,)).astype(jnp.bfloat16)


def code_one_hot(code_block):
    levels = jnp.arange(CENTROIDS, dtype=jnp.int32)
    marked = code_block[:, :, None, :] == levels[None, None, :, None]
    return marked.astype(jnp.bfloat16).reshape(
        code_block.shape[0], SUBSPACES * CENTROIDS, code_block.shape[2]
    )


def group_size(lists_dev, slot_rows):
    group_width = 1
    while (
        group_width * 2 <= lists_dev
        and lists_dev % (group_width * 2) == 0
        and (group_width * slot_rows < 512)
    ):
        group_width = group_width * 2
    return group_width


def first_pass(got_rows, passage_codes, codebook, group_width):
    lists_dev, slot_rows = (got_rows.shape[0], got_rows.shape[1])
    groups = lists_dev // group_width

    def score_piece(pieces):
        row_group, code_group = pieces
        lut_rows = lookup_rows(row_group, codebook)
        one_hot = code_one_hot(code_group)
        scores = jnp.einsum("grk,gkl->grl", lut_rows, one_hot, preferred_element_type=jnp.float32)
        top_score = jnp.max(scores, axis=2)
        exp_total = jnp.sum(jnp.exp(scores - top_score[:, :, None]), axis=2)
        return (scores, top_score, exp_total)

    scores, top_score, exp_total = lax.map(
        score_piece,
        (
            got_rows.reshape(groups, group_width, slot_rows, D),
            passage_codes.reshape(groups, group_width, SUBSPACES, PASSAGES),
        ),
    )
    return (
        scores.reshape(lists_dev, slot_rows, PASSAGES),
        top_score.reshape(lists_dev, slot_rows),
        exp_total.reshape(lists_dev, slot_rows),
    )


def second_pass(
    got_rows, got_notes, passage_codes, codebook, scores, query_top, query_total, group_width
):
    lists_dev, slot_rows = (got_rows.shape[0], got_rows.shape[1])
    groups = lists_dev // group_width
    weights = rank_weights()
    places = jnp.arange(PASSAGES, dtype=jnp.int32)
    centroids = codebook.reshape(CENTROIDS, SUBSPACES, SUBDIM)
    highest = lax.Precision.HIGHEST

    def grad_piece(pieces):
        row_group, note_group, code_group, score_group, top_group, total_group = pieces
        one_hot = code_one_hot(code_group)
        target_spot = note_group[:, :, 1:]
        teacher = jnp.sum(
            jnp.where(target_spot[:, :, :, None] == places, weights[:, None], 0.0), axis=2
        )
        student = jnp.exp(score_group - top_group[:, :, None]) / total_group[:, :, None]
        is_valid = note_group[:, :, 0] >= 0
        grad_scores = jnp.where(is_valid[:, :, None], student - teacher, 0.0).astype(jnp.bfloat16)
        histogram = jnp.einsum(
            "grl,gkl->grk", grad_scores, one_hot, preferred_element_type=jnp.float32
        )
        histogram = histogram.reshape(group_width, slot_rows, SUBSPACES, CENTROIDS)
        partial_value = jnp.einsum("grmk,kme->grme", histogram, centroids, precision=highest)
        split_rows = row_group.astype(jnp.float32).reshape(
            group_width, slot_rows, SUBSPACES, SUBDIM
        )
        book_part = jnp.einsum("grmk,grme->kme", histogram, split_rows, precision=highest)
        return (partial_value.reshape(group_width, slot_rows, D), book_part)

    partial_value, book_part = lax.map(
        grad_piece,
        (
            got_rows.reshape(groups, group_width, slot_rows, D),
            got_notes.reshape(groups, group_width, slot_rows, TARGETS + 1),
            passage_codes.reshape(groups, group_width, SUBSPACES, PASSAGES),
            scores.reshape(groups, group_width, slot_rows, PASSAGES),
            query_top.reshape(groups, group_width, slot_rows),
            query_total.reshape(groups, group_width, slot_rows),
        ),
    )
    return (
        partial_value.reshape(lists_dev, slot_rows, D),
        jnp.sum(book_part, axis=0).reshape(CENTROIDS, D),
    )


def shards(queries, probes, targets, passage_codes, codebook):
    corpus_size = lax.axis_size("corpus")
    query_rows = queries.shape[0]
    lists_dev = passage_codes.shape[0]
    list_total = lists_dev * corpus_size
    capacity = min(query_rows, max(2, 2 * PROBES * query_rows // list_total))
    slot_rows = corpus_size * capacity
    slot_count = lists_dev * slot_rows
    group_width = group_size(lists_dev, slot_rows)
    flat_probes = probes.reshape(-1)
    local_list = flat_probes % lists_dev
    owner_ids = flat_probes // lists_dev
    slot_rank = rank_slots(flat_probes, list_total, jnp.ones(flat_probes.shape, jnp.bool_))
    note_rows = note_block(probes, targets)
    placed = (local_list * corpus_size + owner_ids) * capacity + slot_rank
    sending = (
        jnp.zeros((slot_count, D), jnp.bfloat16).at[placed].set(jnp.repeat(queries, PROBES, axis=0))
    )
    note_buffer = jnp.full((slot_count, TARGETS + 1), -1, jnp.int32).at[placed].set(note_rows)
    got_rows, got_notes = (
        lax.all_to_all(
            sending.reshape(lists_dev, corpus_size, capacity, D),
            "corpus",
            split_axis=1,
            concat_axis=1,
            tiled=True,
        ),
        lax.all_to_all(
            note_buffer.reshape(lists_dev, corpus_size, capacity, TARGETS + 1),
            "corpus",
            split_axis=1,
            concat_axis=1,
            tiled=True,
        ),
    )
    got_rows = got_rows.reshape(lists_dev, slot_rows, D)
    got_notes = got_notes.reshape(lists_dev, slot_rows, TARGETS + 1)
    is_valid = got_notes[:, :, 0] >= 0
    scores, top_score, exp_total = first_pass(got_rows, passage_codes, codebook, group_width)
    top_score = jnp.where(is_valid, top_score, NEGATIVE)
    exp_total = jnp.where(is_valid, exp_total, 0.0)
    back_top, back_total = (
        lax.all_to_all(
            top_score.reshape(lists_dev, corpus_size, capacity),
            "corpus",
            split_axis=1,
            concat_axis=1,
            tiled=True,
        ),
        lax.all_to_all(
            exp_total.reshape(lists_dev, corpus_size, capacity),
            "corpus",
            split_axis=1,
            concat_axis=1,
            tiled=True,
        ),
    )
    entry_top = back_top.reshape(-1)[placed].reshape(query_rows, PROBES)
    entry_total = back_total.reshape(-1)[placed].reshape(query_rows, PROBES)
    own_top = jnp.max(entry_top, axis=1)
    own_total = jnp.sum(entry_total * jnp.exp(entry_top - own_top[:, None]), axis=1)
    slot_top = jnp.zeros((slot_count,), jnp.float32).at[placed].set(jnp.repeat(own_top, PROBES))
    slot_total = jnp.ones((slot_count,), jnp.float32).at[placed].set(jnp.repeat(own_total, PROBES))
    query_top, query_total = (
        lax.all_to_all(
            slot_top.reshape(lists_dev, corpus_size, capacity),
            "corpus",
            split_axis=1,
            concat_axis=1,
            tiled=True,
        ),
        lax.all_to_all(
            slot_total.reshape(lists_dev, corpus_size, capacity),
            "corpus",
            split_axis=1,
            concat_axis=1,
            tiled=True,
        ),
    )
    query_top = query_top.reshape(lists_dev, slot_rows)
    query_total = query_total.reshape(lists_dev, slot_rows)
    query_top = jnp.where(is_valid, query_top, 0.0)
    query_total = jnp.where(is_valid, query_total, 1.0)
    partial_value, book_part = second_pass(
        got_rows, got_notes, passage_codes, codebook, scores, query_top, query_total, group_width
    )
    returned = lax.all_to_all(
        partial_value.reshape(lists_dev, corpus_size, capacity, D),
        "corpus",
        split_axis=1,
        concat_axis=1,
        tiled=True,
    )
    per_probe = returned.reshape(slot_count, D)[placed].reshape(query_rows, PROBES, D)
    grad_queries = jnp.sum(per_probe, axis=1)
    book_sum = lax.psum(book_part, ("corpus", "query"))
    normed = book_sum * lax.rsqrt(jnp.mean(book_sum * book_sum) + EPSILON)
    return (grad_queries.astype(jnp.bfloat16), normed)


def solution(mesh):
    placed = (
        P(("corpus", "query"), None),
        P(("corpus", "query"), None),
        P(("corpus", "query"), None),
        P("corpus", None, None),
        P(),
    )
    return jax.shard_map(
        shards,
        mesh=mesh,
        in_specs=placed,
        out_specs=(P(("corpus", "query"), None), P()),
        check_vma=False,
    )
```

profile of v0, /device:TPU:1, one launch (start us, length us, event | category | flops | bytes accessed | tf_op | source)
XLA Modules:
  0.0 697.2 jit_solution(16750538512104853884)
XLA Ops:
  16.7 9.6 %all-to-all-start = ((s32[32,1,576]{2,1,0:T(1,128)}), s32[32,1,576]{2,1,0:T(1,128)S(1)}, u32[]{:S(2)}, u32[]{:S(2)}) async-start(s32[32,1,576]{2,1,0:T(1,128)} %reshape.393), calls=%async_computation | async-start | bytes 163840 | tf_op jit(solution)/shard_map/all_to_all | solution.py:173
  28.1 7.1 %scatter_custom_fusion.1 = bf16[2048,768]{1,0:T(8,128)(2,1)S(1)} fusion(s32[1024]{0:T(1024)S(1)} %bitcast.179, bf16[1024,768]{1,0:T(8,128)(2,1)} %reshape.360, bf16[]{:T(256)} %constant.118.clone.1), kind=kCustom, calls=%fused_computation.62 | custom fusion | bytes 3146240 | tf_op jit(solution)/shard_map/scatter | solution.py:162
  37.9 6.8 copy.136
  44.7 7.4 %all-to-all-start.1 = ((bf16[32,32,2,768]{3,2,0,1:T(2,128)(2,1)}), bf16[32,32,2,768]{3,2,0,1:T(2,128)(2,1)S(1)}, u32[]{:S(2)}, u32[]{:S(2)}) async-start(bf16[32,32,2,768]{3,2,0,1:T(2,128)(2,1)} %copy.136), calls=%async_computation.1 | async-start | bytes 6291456 | tf_op jit(solution)/shard_map/all_to_all | solution.py:166
  60.2 31.6 %all-to-all-done.1 = bf16[32,32,2,768]{3,2,0,1:T(2,128)(2,1)S(1)} async-done(((bf16[32,32,2,768]{3,2,0,1:T(2,128)(2,1)}), bf16[32,32,2,768]{3,2,0,1:T(2,128)(2,1)S(1)}, u32[]{:S(2)}, u32[]{:S(2)}) %all-to-all-start.1) | async-done | bytes 3145760 | tf_op jit(solution)/shard_map/all_to_all | solution.py:166
  94.2 7.3 %copy.138 = bf16[4,8,64,768]{2,3,1,0:T(8,128)(2,1)} copy(bf16[4,8,64,768]{3,1,0,2:T(8,128)(2,1)} %bitcast.169) | data formatting | bytes 6291456 | tf_op jit(solution)/shard_map/while | solution.py:84
  102.7 129.6 %while.27 = (s32[]{:T(128)}, f32[4,8,64,1024]{3,2,1,0:T(8,128)}, f32[4,8,64]{2,1,0:T(8,128)}, f32[4,8,64]{2,1,0:T(8,128)}, bf16[4,8,64,768]{2,3,1,0:T(8,128)(2,1...) while((s32[]{:T(128)}, f32[4,8,64,1024]{3,2,1,0:T(8,128)}, ...), condition=%wide.region_8.9_spmd, body=%wide.region_5.8_spmd.sunk | while | flops 1701051392 | bytes 57241216 | solution.py:84
  112.8 9.4 %bitcast_compare_fusion.4 = pred[8,1536,1024]{2,1,0:T(32,128)(4,1)} fusion(s32[1536]{0:T(1024)S(1)} %eq.177, s32[8,96,1024]{2,1,0:T(8,128)S(1)} %dynamic-slice_bitcast_fusion.14), kind=kLoop, calls=%fused_computation.9.clone.1 | loop fusion | flops 12582912 | bytes 15734784 | tf_op jit(solution)/shard_map/while/body/eval_jaxpr/eq | solution.py:54
  122.1 11.7 %bitcast_dynamic-update-slice_fusion.5 = (f32[4,8,64,1024]{3,2,1,0:T(8,128)}, f32[8,64,1024]{2,1,0:T(8,128)S(1)}) fusion(f32[4,8,64,1024]{3,2,1,0:T(8,128)} %get-tuple-element.387, s32[]{:T(128)} %get-tuple-element.386, bf16[8,64,1536]{1,2,0:T(8,128)(2,1)S(1)} %bitcast.165, pred[8,1536,1024]{2,1,0:T(32,128)(4,1)} %bitcast_compare_fusion.4), kind=kOutput, calls=%fused_computation.12.clone.1 | convolution fusion | flops 1610612736 | bytes 18350592 | tf_op jit(solution)/shard_map/while/body/eval_jaxpr/grk,gkl->grl/dot_general | solution.py:79
  145.2 9.4 %bitcast_compare_fusion.4 = pred[8,1536,1024]{2,1,0:T(32,128)(4,1)} fusion(s32[1536]{0:T(1024)S(1)} %eq.177, s32[8,96,1024]{2,1,0:T(8,128)S(1)} %dynamic-slice_bitcast_fusion.14), kind=kLoop, calls=%fused_computation.9.clone.1 | loop fusion | flops 12582912 | bytes 15734784 | tf_op jit(solution)/shard_map/while/body/eval_jaxpr/eq | solution.py:54
  154.5 11.7 %bitcast_dynamic-update-slice_fusion.5 = (f32[4,8,64,1024]{3,2,1,0:T(8,128)}, f32[8,64,1024]{2,1,0:T(8,128)S(1)}) fusion(f32[4,8,64,1024]{3,2,1,0:T(8,128)} %get-tuple-element.387, s32[]{:T(128)} %get-tuple-element.386, bf16[8,64,1536]{1,2,0:T(8,128)(2,1)S(1)} %bitcast.165, pred[8,1536,1024]{2,1,0:T(32,128)(4,1)} %bitcast_compare_fusion.4), kind=kOutput, calls=%fused_computation.12.clone.1 | convolution fusion | flops 1610612736 | bytes 18350592 | tf_op jit(solution)/shard_map/while/body/eval_jaxpr/grk,gkl->grl/dot_general | solution.py:79
  177.6 9.4 %bitcast_compare_fusion.4 = pred[8,1536,1024]{2,1,0:T(32,128)(4,1)} fusion(s32[1536]{0:T(1024)S(1)} %eq.177, s32[8,96,1024]{2,1,0:T(8,128)S(1)} %dynamic-slice_bitcast_fusion.14), kind=kLoop, calls=%fused_computation.9.clone.1 | loop fusion | flops 12582912 | bytes 15734784 | tf_op jit(solution)/shard_map/while/body/eval_jaxpr/eq | solution.py:54
  186.9 11.7 %bitcast_dynamic-update-slice_fusion.5 = (f32[4,8,64,1024]{3,2,1,0:T(8,128)}, f32[8,64,1024]{2,1,0:T(8,128)S(1)}) fusion(f32[4,8,64,1024]{3,2,1,0:T(8,128)} %get-tuple-element.387, s32[]{:T(128)} %get-tuple-element.386, bf16[8,64,1536]{1,2,0:T(8,128)(2,1)S(1)} %bitcast.165, pred[8,1536,1024]{2,1,0:T(32,128)(4,1)} %bitcast_compare_fusion.4), kind=kOutput, calls=%fused_computation.12.clone.1 | convolution fusion | flops 1610612736 | bytes 18350592 | tf_op jit(solution)/shard_map/while/body/eval_jaxpr/grk,gkl->grl/dot_general | solution.py:79
  210.0 9.4 %bitcast_compare_fusion.4 = pred[8,1536,1024]{2,1,0:T(32,128)(4,1)} fusion(s32[1536]{0:T(1024)S(1)} %eq.177, s32[8,96,1024]{2,1,0:T(8,128)S(1)} %dynamic-slice_bitcast_fusion.14), kind=kLoop, calls=%fused_computation.9.clone.1 | loop fusion | flops 12582912 | bytes 15734784 | tf_op jit(solution)/shard_map/while/body/eval_jaxpr/eq | solution.py:54
  219.4 11.7 %bitcast_dynamic-update-slice_fusion.5 = (f32[4,8,64,1024]{3,2,1,0:T(8,128)}, f32[8,64,1024]{2,1,0:T(8,128)S(1)}) fusion(f32[4,8,64,1024]{3,2,1,0:T(8,128)} %get-tuple-element.387, s32[]{:T(128)} %get-tuple-element.386, bf16[8,64,1536]{1,2,0:T(8,128)(2,1)S(1)} %bitcast.165, pred[8,1536,1024]{2,1,0:T(32,128)(4,1)} %bitcast_compare_fusion.4), kind=kOutput, calls=%fused_computation.12.clone.1 | convolution fusion | flops 1610612736 | bytes 18350592 | tf_op jit(solution)/shard_map/while/body/eval_jaxpr/grk,gkl->grl/dot_general | solution.py:79
  235.6 11.5 %all_to_all.35 = f32[32,32,2]{0,2,1:T(2,128)S(1)} all-to-all(f32[32,32,2]{0,2,1:T(2,128)S(1)} %get-tuple-element.256), channel_id=1, replica_groups=mesh['corpus'=32,'query'=4] {'corpus'}, dimensions={1} | all-to-all | bytes 16384 | tf_op jit(solution)/shard_map/all_to_all | solution.py:188
  253.0 6.2 gather_fusion
  260.2 6.2 gather_fusion.1
  266.9 4.5 scatter_custom_fusion.3
  272.8 7.5 %all-to-all-start.5 = ((f32[32,32,2]{0,2,1:T(2,128)}), f32[32,32,2]{0,2,1:T(2,128)S(1)}, u32[]{:S(2)}, u32[]{:S(2)}) async-start(f32[32,32,2]{0,2,1:T(2,128)} %copy.148), calls=%async_computation.5 | async-start | bytes 65536 | tf_op jit(solution)/shard_map/all_to_all | solution.py:217
  287.6 6.2 all-to-all-start.3
  295.2 5.9 all-to-all-done.3
  301.3 212.7 %while.28 = (s32[]{:T(128)}, f32[4,8,64,768]{3,1,0,2:T(8,128)}, f32[4,16,96,8]{1,3,2,0:T(8,128)}, s32[4,8,64,9]{2,1,3,0:T(8,128)S(1)}, f32[4,8,64,1024]{3,2,1,0:...) while((s32[]{:T(128)}, f32[4,8,64,768]{3,1,0,2:T(8,128)}, ...), condition=%wide.region_15.16_spmd.clone, body=%wide.region_13.15_spmd.clone.sunk | while | flops 1788871168 | bytes 67385192 | solution.py:129
  302.3 7.1 %select_reduce_fusion.2 = f32[8,64,1024]{2,1,0:T(8,128)} fusion(f32[8]{0:T(128)S(1)} %subtract_multiply_fusion.2, s32[8,64,8]{2,1,0:T(8,128)S(1)} %copy.183), kind=kLoop, calls=%fused_computation.21.clone.1 | loop fusion | flops 12058624 | bytes 2113568 | tf_op jit(solution)/shard_map/while/body/eval_jaxpr/reduce_sum | solution.py:112
  313.6 9.3 %bitcast_compare_fusion.5 = pred[8,1536,1024]{2,1,0:T(32,128)(4,1)} fusion(s32[1536]{0:T(1024)S(1)} %eq.184, s32[8,96,1024]{2,1,0:T(8,128)S(1)} %dynamic-slice_bitcast_fusion.15), kind=kLoop, calls=%fused_computation.19.clone.1 | loop fusion | flops 12582912 | bytes 15734784 | tf_op jit(solution)/shard_map/while/body/eval_jaxpr/eq | solution.py:54
  322.9 12.8 %fusion.84 = f32[8,64,1536]{1,2,0:T(8,128)} fusion(pred[8,1536,1024]{2,1,0:T(32,128)(4,1)} %bitcast_compare_fusion.5, f32[8,64,1024]{2,1,0:T(8,128)} %select_reduce_fusion.2, f32[4,8,64,1024]{3,2,1,0:T(8,128)} %get-tuple-element.430, s32[]{:T(128)} %get-tuple-element.415, f32[8,64]{1,0:T(8,128)S(1)} %get-tuple-element.375, ...), kind=kOutput, calls=%fused_computation.38.clone.1 | convolution fusion | flops 1613234176 | bytes 19928576 | tf_op jit(solution)/shard_map/while/body/eval_jaxpr/grl,gkl->grk/dot_general | solution.py:118
  335.8 5.5 fusion.85
  346.3 8.3 %fusion.86 = f32[4,16,96,8]{1,3,2,0:T(8,128)} fusion(f32[4,16,96,8]{1,3,2,0:T(8,128)} %get-tuple-element.417, s32[]{:T(128)} %get-tuple-element.415, f32[8,64,96,16]{1,3,2,0:T(8,128)} %bitcast.164, bf16[4,8,64,768]{2,3,1,0:T(8,128)(2,1)} %get-tuple-element.435), kind=kOutput, calls=%fused_computation.37.clone.1 | convolution fusion | flops 75497472 | bytes 8258560 | tf_op jit(solution)/shard_map/while/body/eval_jaxpr/grmk,grme->kme/dot_general | solution.py:126
  355.4 7.1 %select_reduce_fusion.2 = f32[8,64,1024]{2,1,0:T(8,128)} fusion(f32[8]{0:T(128)S(1)} %subtract_multiply_fusion.2, s32[8,64,8]{2,1,0:T(8,128)S(1)} %copy.183), kind=kLoop, calls=%fused_computation.21.clone.1 | loop fusion | flops 12058624 | bytes 2113568 | tf_op jit(solution)/shard_map/while/body/eval_jaxpr/reduce_sum | solution.py:112
  366.7 9.3 %bitcast_compare_fusion.5 = pred[8,1536,1024]{2,1,0:T(32,128)(4,1)} fusion(s32[1536]{0:T(1024)S(1)} %eq.184, s32[8,96,1024]{2,1,0:T(8,128)S(1)} %dynamic-slice_bitcast_fusion.15), kind=kLoop, calls=%fused_computation.19.clone.1 | loop fusion | flops 12582912 | bytes 15734784 | tf_op jit(solution)/shard_map/while/body/eval_jaxpr/eq | solution.py:54
  376.0 12.8 %fusion.84 = f32[8,64,1536]{1,2,0:T(8,128)} fusion(pred[8,1536,1024]{2,1,0:T(32,128)(4,1)} %bitcast_compare_fusion.5, f32[8,64,1024]{2,1,0:T(8,128)} %select_reduce_fusion.2, f32[4,8,64,1024]{3,2,1,0:T(8,128)} %get-tuple-element.430, s32[]{:T(128)} %get-tuple-element.415, f32[8,64]{1,0:T(8,128)S(1)} %get-tuple-element.375, ...), kind=kOutput, calls=%fused_computation.38.clone.1 | convolution fusion | flops 1613234176 | bytes 19928576 | tf_op jit(solution)/shard_map/while/body/eval_jaxpr/grl,gkl->grk/dot_general | solution.py:118
  388.9 5.5 fusion.85
  399.4 8.2 %fusion.86 = f32[4,16,96,8]{1,3,2,0:T(8,128)} fusion(f32[4,16,96,8]{1,3,2,0:T(8,128)} %get-tuple-element.417, s32[]{:T(128)} %get-tuple-element.415, f32[8,64,96,16]{1,3,2,0:T(8,128)} %bitcast.164, bf16[4,8,64,768]{2,3,1,0:T(8,128)(2,1)} %get-tuple-element.435), kind=kOutput, calls=%fused_computation.37.clone.1 | convolution fusion | flops 75497472 | bytes 8258560 | tf_op jit(solution)/shard_map/while/body/eval_jaxpr/grmk,grme->kme/dot_general | solution.py:126
  408.4 7.1 %select_reduce_fusion.2 = f32[8,64,1024]{2,1,0:T(8,128)} fusion(f32[8]{0:T(128)S(1)} %subtract_multiply_fusion.2, s32[8,64,8]{2,1,0:T(8,128)S(1)} %copy.183), kind=kLoop, calls=%fused_computation.21.clone.1 | loop fusion | flops 12058624 | bytes 2113568 | tf_op jit(solution)/shard_map/while/body/eval_jaxpr/reduce_sum | solution.py:112
  419.8 9.3 %bitcast_compare_fusion.5 = pred[8,1536,1024]{2,1,0:T(32,128)(4,1)} fusion(s32[1536]{0:T(1024)S(1)} %eq.184, s32[8,96,1024]{2,1,0:T(8,128)S(1)} %dynamic-slice_bitcast_fusion.15), kind=kLoop, calls=%fused_computation.19.clone.1 | loop fusion | flops 12582912 | bytes 15734784 | tf_op jit(solution)/shard_map/while/body/eval_jaxpr/eq | solution.py:54
  429.1 12.8 %fusion.84 = f32[8,64,1536]{1,2,0:T(8,128)} fusion(pred[8,1536,1024]{2,1,0:T(32,128)(4,1)} %bitcast_compare_fusion.5, f32[8,64,1024]{2,1,0:T(8,128)} %select_reduce_fusion.2, f32[4,8,64,1024]{3,2,1,0:T(8,128)} %get-tuple-element.430, s32[]{:T(128)} %get-tuple-element.415, f32[8,64]{1,0:T(8,128)S(1)} %get-tuple-element.375, ...), kind=kOutput, calls=%fused_computation.38.clone.1 | convolution fusion | flops 1613234176 | bytes 19928576 | tf_op jit(solution)/shard_map/while/body/eval_jaxpr/grl,gkl->grk/dot_general | solution.py:118
  441.9 5.5 fusion.85
  452.5 8.2 %fusion.86 = f32[4,16,96,8]{1,3,2,0:T(8,128)} fusion(f32[4,16,96,8]{1,3,2,0:T(8,128)} %get-tuple-element.417, s32[]{:T(128)} %get-tuple-element.415, f32[8,64,96,16]{1,3,2,0:T(8,128)} %bitcast.164, bf16[4,8,64,768]{2,3,1,0:T(8,128)(2,1)} %get-tuple-element.435), kind=kOutput, calls=%fused_computation.37.clone.1 | convolution fusion | flops 75497472 | bytes 8258560 | tf_op jit(solution)/shard_map/while/body/eval_jaxpr/grmk,grme->kme/dot_general | solution.py:126
  461.5 7.1 %select_reduce_fusion.2 = f32[8,64,1024]{2,1,0:T(8,128)} fusion(f32[8]{0:T(128)S(1)} %subtract_multiply_fusion.2, s32[8,64,8]{2,1,0:T(8,128)S(1)} %copy.183), kind=kLoop, calls=%fused_computation.21.clone.1 | loop fusion | flops 12058624 | bytes 2113568 | tf_op jit(solution)/shard_map/while/body/eval_jaxpr/reduce_sum | solution.py:112
  472.8 9.3 %bitcast_compare_fusion.5 = pred[8,1536,1024]{2,1,0:T(32,128)(4,1)} fusion(s32[1536]{0:T(1024)S(1)} %eq.184, s32[8,96,1024]{2,1,0:T(8,128)S(1)} %dynamic-slice_bitcast_fusion.15), kind=kLoop, calls=%fused_computation.19.clone.1 | loop fusion | flops 12582912 | bytes 15734784 | tf_op jit(solution)/shard_map/while/body/eval_jaxpr/eq | solution.py:54
  482.2 12.8 %fusion.84 = f32[8,64,1536]{1,2,0:T(8,128)} fusion(pred[8,1536,1024]{2,1,0:T(32,128)(4,1)} %bitcast_compare_fusion.5, f32[8,64,1024]{2,1,0:T(8,128)} %select_reduce_fusion.2, f32[4,8,64,1024]{3,2,1,0:T(8,128)} %get-tuple-element.430, s32[]{:T(128)} %get-tuple-element.415, f32[8,64]{1,0:T(8,128)S(1)} %get-tuple-element.375, ...), kind=kOutput, calls=%fused_computation.38.clone.1 | convolution fusion | flops 1613234176 | bytes 19928576 | tf_op jit(solution)/shard_map/while/body/eval_jaxpr/grl,gkl->grk/dot_general | solution.py:118
  495.0 5.5 fusion.85
  505.6 8.2 %fusion.86 = f32[4,16,96,8]{1,3,2,0:T(8,128)} fusion(f32[4,16,96,8]{1,3,2,0:T(8,128)} %get-tuple-element.417, s32[]{:T(128)} %get-tuple-element.415, f32[8,64,96,16]{1,3,2,0:T(8,128)} %bitcast.164, bf16[4,8,64,768]{2,3,1,0:T(8,128)(2,1)} %get-tuple-element.435), kind=kOutput, calls=%fused_computation.37.clone.1 | convolution fusion | flops 75497472 | bytes 8258560 | tf_op jit(solution)/shard_map/while/body/eval_jaxpr/grmk,grme->kme/dot_general | solution.py:126
  514.1 5.0 all-to-all-start.6
  519.2 141.8 %psum.7 = f32[16,768]{0,1:T(8,128)S(1)} all-reduce(f32[16,768]{0,1:T(8,128)S(1)} %bitcast.174), channel_id=1, replica_groups=mesh['corpus'=32,'query'=4] {'corpus','query'}, use_global_device_ids=true, to_apply=%region_18.19 | all-reduce | flops 12288 | bytes 98304 | tf_op jit(solution)/shard_map/psum | solution.py:241
  663.2 10.3 %copy.154 = f32[32,32,2,768]{3,2,1,0:T(2,128)} copy(f32[32,32,2,768]{3,0,2,1:T(8,128)} %all-to-all-done.6) | data formatting | bytes 12582912 | tf_op jit(solution)/shard_map/all_to_all | solution.py:232
  673.5 8.5 %reshape.321 = f32[2048,768]{1,0:T(8,128)} reshape(f32[32,32,2,768]{3,2,1,0:T(2,128)} %copy.154) | data formatting | bytes 12582912 | tf_op jit(solution)/shard_map/reshape | solution.py:239
  682.1 8.7 %gather_fusion.2 = f32[1024,768]{1,0:T(8,128)} fusion(f32[2048,768]{1,0:T(8,128)} %reshape.321, s32[1024]{0:T(1024)S(1)} %copy-done.14), kind=kCustom, calls=%fused_computation.2 | custom fusion | bytes 6295552 | tf_op jit(solution)/shard_map/gather | solution.py:239
  (241 shorter events, 145.7 us)
Async XLA Ops:
  2.4 1.9 copy-start.1
  9.5 0.8 copy-start.16
  10.2 16.1 %copy-start.7 = (bf16[256,768]{1,0:T(8,128)(2,1)S(1)}, bf16[256,768]{1,0:T(8,128)(2,1)}, u32[]{:S(2)}) copy-start(bf16[256,768]{1,0:T(8,128)(2,1)} %param.9) | copy-start | bytes 1179652
  10.9 17.1 %copy-start.15 = (s32[1024,1]{0,1:T(1,128)}, s32[1024,1]{0,1:T(1,128)S(1)}, u32[]{:S(2)}) copy-start(s32[1024,1]{0,1:T(1,128)S(1)} %compare_select_fusion.1) | copy-start | bytes 12292
  16.7 28.0 %all-to-all-start = ((s32[32,1,576]{2,1,0:T(1,128)}), s32[32,1,576]{2,1,0:T(1,128)S(1)}, u32[]{:S(2)}, u32[]{:S(2)}) async-start(s32[32,1,576]{2,1,0:T(1,128)} %reshape.393), calls=%async_computation | async-start | bytes 163840 | tf_op jit(solution)/shard_map/all_to_all | solution.py:173
  44.7 7.4 %copy-start.8 = (s32[32,1,576]{2,1,0:T(1,128)}, s32[32,1,576]{2,1,0:T(1,128)S(1)}, u32[]{:S(2)}) copy-start(s32[32,1,576]{2,1,0:T(1,128)S(1)} %all-to-all-done) | copy-start | bytes 221188
  44.7 47.1 %all-to-all-start.1 = ((bf16[32,32,2,768]{3,2,0,1:T(2,128)(2,1)}), bf16[32,32,2,768]{3,2,0,1:T(2,128)(2,1)S(1)}, u32[]{:S(2)}, u32[]{:S(2)}) async-start(bf16[32,32,2,768]{3,2,0,1:T(2,128)(2,1)} %copy.136), calls=%async_computation.1 | async-start | bytes 6291456 | tf_op jit(solution)/shard_map/all_to_all | solution.py:166
  58.8 0.7 copy-start.3
  112.8 9.4 %copy-start = (bf16[8,64,96,16]{1,3,2,0:T(8,128)(2,1)S(1)}, bf16[8,64,96,16]{1,3,2,0:T(8,128)(2,1)}, u32[]{:S(2)}) copy-start(bf16[8,64,96,16]{1,3,2,0:T(8,128)(2,1)} %copy.181) | copy-start | bytes 4718596 | tf_op jit(solution)/shard_map/while
  145.2 9.4 %copy-start = (bf16[8,64,96,16]{1,3,2,0:T(8,128)(2,1)S(1)}, bf16[8,64,96,16]{1,3,2,0:T(8,128)(2,1)}, u32[]{:S(2)}) copy-start(bf16[8,64,96,16]{1,3,2,0:T(8,128)(2,1)} %copy.181) | copy-start | bytes 4718596 | tf_op jit(solution)/shard_map/while
  177.6 9.4 %copy-start = (bf16[8,64,96,16]{1,3,2,0:T(8,128)(2,1)S(1)}, bf16[8,64,96,16]{1,3,2,0:T(8,128)(2,1)}, u32[]{:S(2)}) copy-start(bf16[8,64,96,16]{1,3,2,0:T(8,128)(2,1)} %copy.181) | copy-start | bytes 4718596 | tf_op jit(solution)/shard_map/while
  210.0 9.4 %copy-start = (bf16[8,64,96,16]{1,3,2,0:T(8,128)(2,1)S(1)}, bf16[8,64,96,16]{1,3,2,0:T(8,128)(2,1)}, u32[]{:S(2)}) copy-start(bf16[8,64,96,16]{1,3,2,0:T(8,128)(2,1)} %copy.181) | copy-start | bytes 4718596 | tf_op jit(solution)/shard_map/while
  247.1 12.3 %all-to-all-start.4 = ((f32[32,32,2]{0,2,1:T(2,128)}), f32[32,32,2]{0,2,1:T(2,128)S(1)}, u32[]{:S(2)}, u32[]{:S(2)}) async-start(f32[32,32,2]{0,2,1:T(2,128)} %get-tuple-element.255), calls=%async_computation.4 | async-start | bytes 65536 | tf_op jit(solution)/shard_map/all_to_all | solution.py:195
  252.2 14.2 %copy-start.13 = (s32[1024]{0:T(1024)}, s32[1024]{0:T(1024)S(1)}, u32[]{:S(2)}) copy-start(s32[1024]{0:T(1024)S(1)} %broadcast_clamp_fusion) | copy-start | bytes 12292
  259.4 34.5 %copy-start.4 = (s32[32,32,2,9]{0,2,1,3:T(2,128)S(1)}, s32[32,32,2,9]{0,2,1,3:T(2,128)}, u32[]{:S(2)}) copy-start(s32[32,32,2,9]{0,2,1,3:T(2,128)} %copy-done.3) | copy-start | bytes 221188
  272.8 14.8 %all-to-all-start.5 = ((f32[32,32,2]{0,2,1:T(2,128)}), f32[32,32,2]{0,2,1:T(2,128)S(1)}, u32[]{:S(2)}, u32[]{:S(2)}) async-start(f32[32,32,2]{0,2,1:T(2,128)} %copy.148), calls=%async_computation.5 | async-start | bytes 65536 | tf_op jit(solution)/shard_map/all_to_all | solution.py:217
  287.6 13.5 %all-to-all-start.3 = ((f32[32,32,2]{0,2,1:T(2,128)}), f32[32,32,2]{0,2,1:T(2,128)S(1)}, u32[]{:S(2)}, u32[]{:S(2)}) async-start(f32[32,32,2]{0,2,1:T(2,128)} %copy.144), calls=%async_computation.3 | async-start | bytes 65536 | tf_op jit(solution)/shard_map/all_to_all | solution.py:210
  301.5 0.6 copy-start.9
  301.5 0.6 copy-start.11
  301.5 8.5 %copy-start.5 = (s32[4,8,64,9]{2,1,3,0:T(8,128)}, s32[4,8,64,9]{2,1,3,0:T(8,128)S(1)}, u32[]{:S(2)}) copy-start(s32[4,8,64,9]{2,1,3,0:T(8,128)S(1)} %get-tuple-element.429) | copy-start | bytes 221188 | tf_op jit(solution)/shard_map/while
  346.3 8.3 %copy-start.6 = (s32[4,8,64,9]{2,1,3,0:T(8,128)S(1)}, s32[4,8,64,9]{2,1,3,0:T(8,128)}, u32[]{:S(2)}) copy-start(s32[4,8,64,9]{2,1,3,0:T(8,128)} %copy-done.5) | copy-start | bytes 221188 | tf_op jit(solution)/shard_map/while
  346.3 8.3 %copy-start.10 = (f32[4,8,64]{2,1,0:T(8,128)S(1)}, f32[4,8,64]{2,1,0:T(8,128)}, u32[]{:S(2)}) copy-start(f32[4,8,64]{2,1,0:T(8,128)} %copy-done.9) | copy-start | bytes 24580 | tf_op jit(solution)/shard_map/while
  346.3 8.3 %copy-start.12 = (f32[4,8,64]{2,1,0:T(8,128)S(1)}, f32[4,8,64]{2,1,0:T(8,128)}, u32[]{:S(2)}) copy-start(f32[4,8,64]{2,1,0:T(8,128)} %copy-done.11) | copy-start | bytes 24580 | tf_op jit(solution)/shard_map/while
  354.6 0.6 copy-start.9
  354.6 0.6 copy-start.11
  354.6 8.5 %copy-start.5 = (s32[4,8,64,9]{2,1,3,0:T(8,128)}, s32[4,8,64,9]{2,1,3,0:T(8,128)S(1)}, u32[]{:S(2)}) copy-start(s32[4,8,64,9]{2,1,3,0:T(8,128)S(1)} %get-tuple-element.429) | copy-start | bytes 221188 | tf_op jit(solution)/shard_map/while
  399.4 8.2 %copy-start.6 = (s32[4,8,64,9]{2,1,3,0:T(8,128)S(1)}, s32[4,8,64,9]{2,1,3,0:T(8,128)}, u32[]{:S(2)}) copy-start(s32[4,8,64,9]{2,1,3,0:T(8,128)} %copy-done.5) | copy-start | bytes 221188 | tf_op jit(solution)/shard_map/while
  399.4 8.2 %copy-start.10 = (f32[4,8,64]{2,1,0:T(8,128)S(1)}, f32[4,8,64]{2,1,0:T(8,128)}, u32[]{:S(2)}) copy-start(f32[4,8,64]{2,1,0:T(8,128)} %copy-done.9) | copy-start | bytes 24580 | tf_op jit(solution)/shard_map/while
  399.4 8.2 %copy-start.12 = (f32[4,8,64]{2,1,0:T(8,128)S(1)}, f32[4,8,64]{2,1,0:T(8,128)}, u32[]{:S(2)}) copy-start(f32[4,8,64]{2,1,0:T(8,128)} %copy-done.11) | copy-start | bytes 24580 | tf_op jit(solution)/shard_map/while
  407.7 0.6 copy-start.9
  407.7 0.6 copy-start.11
  407.7 8.5 %copy-start.5 = (s32[4,8,64,9]{2,1,3,0:T(8,128)}, s32[4,8,64,9]{2,1,3,0:T(8,128)S(1)}, u32[]{:S(2)}) copy-start(s32[4,8,64,9]{2,1,3,0:T(8,128)S(1)} %get-tuple-element.429) | copy-start | bytes 221188 | tf_op jit(solution)/shard_map/while
  452.5 8.3 %copy-start.6 = (s32[4,8,64,9]{2,1,3,0:T(8,128)S(1)}, s32[4,8,64,9]{2,1,3,0:T(8,128)}, u32[]{:S(2)}) copy-start(s32[4,8,64,9]{2,1,3,0:T(8,128)} %copy-done.5) | copy-start | bytes 221188 | tf_op jit(solution)/shard_map/while
  452.5 8.3 %copy-start.10 = (f32[4,8,64]{2,1,0:T(8,128)S(1)}, f32[4,8,64]{2,1,0:T(8,128)}, u32[]{:S(2)}) copy-start(f32[4,8,64]{2,1,0:T(8,128)} %copy-done.9) | copy-start | bytes 24580 | tf_op jit(solution)/shard_map/while
  452.5 8.3 %copy-start.12 = (f32[4,8,64]{2,1,0:T(8,128)S(1)}, f32[4,8,64]{2,1,0:T(8,128)}, u32[]{:S(2)}) copy-start(f32[4,8,64]{2,1,0:T(8,128)} %copy-done.11) | copy-start | bytes 24580 | tf_op jit(solution)/shard_map/while
  460.7 0.6 copy-start.9
  460.8 0.6 copy-start.11
  460.8 8.5 %copy-start.5 = (s32[4,8,64,9]{2,1,3,0:T(8,128)}, s32[4,8,64,9]{2,1,3,0:T(8,128)S(1)}, u32[]{:S(2)}) copy-start(s32[4,8,64,9]{2,1,3,0:T(8,128)S(1)} %get-tuple-element.429) | copy-start | bytes 221188 | tf_op jit(solution)/shard_map/while
  505.6 8.2 %copy-start.6 = (s32[4,8,64,9]{2,1,3,0:T(8,128)S(1)}, s32[4,8,64,9]{2,1,3,0:T(8,128)}, u32[]{:S(2)}) copy-start(s32[4,8,64,9]{2,1,3,0:T(8,128)} %copy-done.5) | copy-start | bytes 221188 | tf_op jit(solution)/shard_map/while
  505.6 8.2 %copy-start.10 = (f32[4,8,64]{2,1,0:T(8,128)S(1)}, f32[4,8,64]{2,1,0:T(8,128)}, u32[]{:S(2)}) copy-start(f32[4,8,64]{2,1,0:T(8,128)} %copy-done.9) | copy-start | bytes 24580 | tf_op jit(solution)/shard_map/while
  505.6 8.2 %copy-start.12 = (f32[4,8,64]{2,1,0:T(8,128)S(1)}, f32[4,8,64]{2,1,0:T(8,128)}, u32[]{:S(2)}) copy-start(f32[4,8,64]{2,1,0:T(8,128)} %copy-done.11) | copy-start | bytes 24580 | tf_op jit(solution)/shard_map/while
  514.0 5.0 copy-start.2
  514.1 149.2 %all-to-all-start.6 = ((f32[32,32,2,768]{3,0,2,1:T(8,128)}), f32[32,32,2,768]{3,0,2,1:T(8,128)}, u32[]{:S(2)}, u32[]{:S(2)}) async-start(f32[32,32,2,768]{3,0,2,1:T(8,128)} %bitcast.170), calls=%async_computation.6 | async-start | bytes 12582912 | tf_op jit(solution)/shard_map/all_to_all | solution.py:232
  673.5 8.5 %copy-start.14 = (s32[1024]{0:T(1024)S(1)}, s32[1024]{0:T(1024)}, u32[]{:S(2)}) copy-start(s32[1024]{0:T(1024)} %copy-done.13) | copy-start | bytes 12292
where the time goes:
time: 708 us; the launch traced here: 697 us
  matrix products  170 us (24%)
  local copies, waits for them, and re-layouts  168 us (24%)
  blocking collectives  153 us (22%)
  other arithmetic  125 us (18%)
  starting transfers between devices  40.1 us (6%)
  waiting for transfers between devices  38.7 us (5%)
    psum x1, blocking collectives, shards(): book_sum = lax.psum(book_part, ('corpus', 'query'))  142 us
    eq x8, other arithmetic, code_one_hot(): marked = code_block[:, :, None, :] == levels[None, None, :, None]  74.8 us
    dot_general x4, matrix products, grad_piece(): jnp.einsum('grl,gkl->grk', grad_scores, one_hot, preferred_element_type=j...  51.3 us
    dot_general x4, matrix products, score_piece(): jnp.einsum('grk,gkl->grl', lut_rows, one_hot, preferred_element_type=jnp....  46.8 us
    dot_general x4, matrix products, grad_piece(): jnp.einsum('grmk,grme->kme', histogram, split_rows, precision=highest)  33 us
    all_to_all x1, waiting for transfers between devices, shards(): lax.all_to_all(sending.reshape(lists_dev, corpus_size, capacity, D), 'cor...  31.6 us
    eq x24, local copies, waits for them, and re-layouts, code_one_hot(): marked = code_block[:, :, None, :] == levels[None, None, :, None]  28.9 us
    reduce_sum x4, other arithmetic, grad_piece(): jnp.sum(jnp.where(target_spot[:, :, :, None] == places, weights[:, None],...  28.5 us
  transfers between devices with their start and end apart: 6, of which 3 were waited for; matrix products, arithmetic and copies ran while one was open for 6% of the time, Pallas kernels for 0%

commit v1 on v0

--- a/solution.py
+++ b/solution.py
@@ -238,7 +238,8 @@
     )
     per_probe = returned.reshape(slot_count, D)[placed].reshape(query_rows, PROBES, D)
     grad_queries = jnp.sum(per_probe, axis=1)
-    book_sum = lax.psum(book_part, ("corpus", "query"))
+    terms = lax.all_gather(book_part, ("corpus", "query"))
+    book_sum = jnp.sum(terms, axis=0)
     normed = book_sum * lax.rsqrt(jnp.mean(book_sum * book_sum) + EPSILON)
     return (grad_queries.astype(jnp.bfloat16), normed)
 

time: 708 us -> 662 us (0.935)
  blocking collectives: 153 us -> 96.4 us
  between operations: 2.26 us -> 15.6 us
    psum x1 -> x0, blocking collectives: 142 us -> none  [shards(): book_sum = lax.psum(book_part, ('corpus', 'query'))]
    all_to_all x0 -> x1, blocking collectives: none -> 84.9 us  [shards(): lax.all_to_all(partial_value.reshape(lists_dev, corpus_size, capacity, D)...]
  transfers between devices with their start and end apart: 6 -> 6, of which waited for: 3 -> 3; matrix products, arithmetic and copies ran while one was open for 6% -> 11% of each run, Pallas kernels for 0% -> 0%
where the time goes in v1:
time: 662 us; the launch traced here: 651 us
  matrix products  170 us (26%)
  local copies, waits for them, and re-layouts  166 us (25%)
  other arithmetic  129 us (19%)
  blocking collectives  96.4 us (15%)
  waiting for transfers between devices  38.5 us (6%)
  starting transfers between devices  35.6 us (5%)
  between operations  15.6 us (2%)
    all_to_all x1, blocking collectives, shards(): lax.all_to_all(partial_value.reshape(lists_dev, corpus_size, capacity, D)...  84.9 us
    eq x8, other arithmetic, code_one_hot(): marked = code_block[:, :, None, :] == levels[None, None, :, None]  74.8 us
    dot_general x4, matrix products, grad_piece(): jnp.einsum('grl,gkl->grk', grad_scores, one_hot, preferred_element_type=j...  51.2 us
    dot_general x4, matrix products, score_piece(): jnp.einsum('grk,gkl->grl', lut_rows, one_hot, preferred_element_type=jnp....  46.8 us
    dot_general x4, matrix products, grad_piece(): jnp.einsum('grmk,grme->kme', histogram, split_rows, precision=highest)  33 us
    all_to_all x1, waiting for transfers between devices, shards(): lax.all_to_all(sending.reshape(lists_dev, corpus_size, capacity, D), 'cor...  31.4 us
    eq x24, local copies, waits for them, and re-layouts, code_one_hot(): marked = code_block[:, :, None, :] == levels[None, None, :, None]  28.9 us
    reduce_sum x4, other arithmetic, grad_piece(): jnp.sum(jnp.where(target_spot[:, :, :, None] == places, weights[:, None],...  28.5 us
  transfers between devices with their start and end apart: 6, of which 3 were waited for; matrix products, arithmetic and copies ran while one was open for 11% of the time, Pallas kernels for 0%

profile of v1, /device:TPU:1, one launch (start us, length us, event | category | flops | bytes accessed | tf_op | source)
XLA Modules:
  0.0 651.4 jit_solution(3782662700504887091)
XLA Ops:
  23.2 9.6 %all-to-all-start = ((s32[32,1,576]{2,1,0:T(1,128)}), s32[32,1,576]{2,1,0:T(1,128)S(1)}, u32[]{:S(2)}, u32[]{:S(2)}) async-start(s32[32,1,576]{2,1,0:T(1,128)} %reshape.389), calls=%async_computation | async-start | bytes 163840 | tf_op jit(solution)/shard_map/all_to_all | solution.py:173
  34.6 7.1 %scatter_custom_fusion.1 = bf16[2048,768]{1,0:T(8,128)(2,1)S(1)} fusion(s32[1024]{0:T(1024)S(1)} %bitcast.179, bf16[1024,768]{1,0:T(8,128)(2,1)} %reshape.356, bf16[]{:T(256)} %constant.118.clone.1), kind=kCustom, calls=%fused_computation.62 | custom fusion | bytes 3146240 | tf_op jit(solution)/shard_map/scatter | solution.py:162
  44.4 6.8 %copy.136 = bf16[32,32,2,768]{3,2,0,1:T(2,128)(2,1)} copy(bf16[32,32,2,768]{3,2,1,0:T(2,128)(2,1)} %reshape.302) | data formatting | bytes 6291456 | tf_op jit(solution)/shard_map/reshape | solution.py:167
  51.2 7.7 %all-to-all-start.1 = ((bf16[32,32,2,768]{3,2,0,1:T(2,128)(2,1)}), bf16[32,32,2,768]{3,2,0,1:T(2,128)(2,1)S(1)}, u32[]{:S(2)}, u32[]{:S(2)}) async-start(bf16[32,32,2,768]{3,2,0,1:T(2,128)(2,1)} %copy.136), calls=%async_computation.1 | async-start | bytes 6291456 | tf_op jit(solution)/shard_map/all_to_all | solution.py:166
  67.1 31.4 %all-to-all-done.1 = bf16[32,32,2,768]{3,2,0,1:T(2,128)(2,1)S(1)} async-done(((bf16[32,32,2,768]{3,2,0,1:T(2,128)(2,1)}), bf16[32,32,2,768]{3,2,0,1:T(2,128)(2,1)S(1)}, u32[]{:S(2)}, u32[]{:S(2)}) %all-to-all-start.1) | async-done | bytes 3145760 | tf_op jit(solution)/shard_map/all_to_all | solution.py:166
  100.9 7.3 %copy.138 = bf16[4,8,64,768]{2,3,1,0:T(8,128)(2,1)} copy(bf16[4,8,64,768]{3,1,0,2:T(8,128)(2,1)} %bitcast.169) | data formatting | bytes 6291456 | tf_op jit(solution)/shard_map/while | solution.py:84
  109.4 129.6 %while.27 = (s32[]{:T(128)}, f32[4,8,64,1024]{3,2,1,0:T(8,128)}, f32[4,8,64]{2,1,0:T(8,128)}, f32[4,8,64]{2,1,0:T(8,128)}, bf16[4,8,64,768]{2,3,1,0:T(8,128)(2,1...) while((s32[]{:T(128)}, f32[4,8,64,1024]{3,2,1,0:T(8,128)}, ...), condition=%wide.region_8.9_spmd, body=%wide.region_5.8_spmd.sunk | while | flops 1701051392 | bytes 57241216 | solution.py:84
  119.5 9.4 %bitcast_compare_fusion.4 = pred[8,1536,1024]{2,1,0:T(32,128)(4,1)} fusion(s32[1536]{0:T(1024)S(1)} %eq.177, s32[8,96,1024]{2,1,0:T(8,128)S(1)} %dynamic-slice_bitcast_fusion.14), kind=kLoop, calls=%fused_computation.9.clone.1 | loop fusion | flops 12582912 | bytes 15734784 | tf_op jit(solution)/shard_map/while/body/eval_jaxpr/eq | solution.py:54
  128.8 11.7 %bitcast_dynamic-update-slice_fusion.5 = (f32[4,8,64,1024]{3,2,1,0:T(8,128)}, f32[8,64,1024]{2,1,0:T(8,128)S(1)}) fusion(f32[4,8,64,1024]{3,2,1,0:T(8,128)} %get-tuple-element.383, s32[]{:T(128)} %get-tuple-element.382, bf16[8,64,1536]{1,2,0:T(8,128)(2,1)S(1)} %bitcast.165, pred[8,1536,1024]{2,1,0:T(32,128)(4,1)} %bitcast_compare_fusion.4), kind=kOutput, calls=%fused_computation.12.clone.1 | convolution fusion | flops 1610612736 | bytes 18350592 | tf_op jit(solution)/shard_map/while/body/eval_jaxpr/grk,gkl->grl/dot_general | solution.py:79
  151.9 9.4 %bitcast_compare_fusion.4 = pred[8,1536,1024]{2,1,0:T(32,128)(4,1)} fusion(s32[1536]{0:T(1024)S(1)} %eq.177, s32[8,96,1024]{2,1,0:T(8,128)S(1)} %dynamic-slice_bitcast_fusion.14), kind=kLoop, calls=%fused_computation.9.clone.1 | loop fusion | flops 12582912 | bytes 15734784 | tf_op jit(solution)/shard_map/while/body/eval_jaxpr/eq | solution.py:54
  161.3 11.7 %bitcast_dynamic-update-slice_fusion.5 = (f32[4,8,64,1024]{3,2,1,0:T(8,128)}, f32[8,64,1024]{2,1,0:T(8,128)S(1)}) fusion(f32[4,8,64,1024]{3,2,1,0:T(8,128)} %get-tuple-element.383, s32[]{:T(128)} %get-tuple-element.382, bf16[8,64,1536]{1,2,0:T(8,128)(2,1)S(1)} %bitcast.165, pred[8,1536,1024]{2,1,0:T(32,128)(4,1)} %bitcast_compare_fusion.4), kind=kOutput, calls=%fused_computation.12.clone.1 | convolution fusion | flops 1610612736 | bytes 18350592 | tf_op jit(solution)/shard_map/while/body/eval_jaxpr/grk,gkl->grl/dot_general | solution.py:79
  184.3 9.4 %bitcast_compare_fusion.4 = pred[8,1536,1024]{2,1,0:T(32,128)(4,1)} fusion(s32[1536]{0:T(1024)S(1)} %eq.177, s32[8,96,1024]{2,1,0:T(8,128)S(1)} %dynamic-slice_bitcast_fusion.14), kind=kLoop, calls=%fused_computation.9.clone.1 | loop fusion | flops 12582912 | bytes 15734784 | tf_op jit(solution)/shard_map/while/body/eval_jaxpr/eq | solution.py:54
  193.7 11.7 %bitcast_dynamic-update-slice_fusion.5 = (f32[4,8,64,1024]{3,2,1,0:T(8,128)}, f32[8,64,1024]{2,1,0:T(8,128)S(1)}) fusion(f32[4,8,64,1024]{3,2,1,0:T(8,128)} %get-tuple-element.383, s32[]{:T(128)} %get-tuple-element.382, bf16[8,64,1536]{1,2,0:T(8,128)(2,1)S(1)} %bitcast.165, pred[8,1536,1024]{2,1,0:T(32,128)(4,1)} %bitcast_compare_fusion.4), kind=kOutput, calls=%fused_computation.12.clone.1 | convolution fusion | flops 1610612736 | bytes 18350592 | tf_op jit(solution)/shard_map/while/body/eval_jaxpr/grk,gkl->grl/dot_general | solution.py:79
  216.7 9.4 %bitcast_compare_fusion.4 = pred[8,1536,1024]{2,1,0:T(32,128)(4,1)} fusion(s32[1536]{0:T(1024)S(1)} %eq.177, s32[8,96,1024]{2,1,0:T(8,128)S(1)} %dynamic-slice_bitcast_fusion.14), kind=kLoop, calls=%fused_computation.9.clone.1 | loop fusion | flops 12582912 | bytes 15734784 | tf_op jit(solution)/shard_map/while/body/eval_jaxpr/eq | solution.py:54
  226.1 11.7 %bitcast_dynamic-update-slice_fusion.5 = (f32[4,8,64,1024]{3,2,1,0:T(8,128)}, f32[8,64,1024]{2,1,0:T(8,128)S(1)}) fusion(f32[4,8,64,1024]{3,2,1,0:T(8,128)} %get-tuple-element.383, s32[]{:T(128)} %get-tuple-element.382, bf16[8,64,1536]{1,2,0:T(8,128)(2,1)S(1)} %bitcast.165, pred[8,1536,1024]{2,1,0:T(32,128)(4,1)} %bitcast_compare_fusion.4), kind=kOutput, calls=%fused_computation.12.clone.1 | convolution fusion | flops 1610612736 | bytes 18350592 | tf_op jit(solution)/shard_map/while/body/eval_jaxpr/grk,gkl->grl/dot_general | solution.py:79
  242.3 11.5 %all_to_all.35 = f32[32,32,2]{0,2,1:T(2,128)S(1)} all-to-all(f32[32,32,2]{0,2,1:T(2,128)S(1)} %get-tuple-element.252), channel_id=1, replica_groups=mesh['corpus'=32,'query'=4] {'corpus'}, dimensions={1} | all-to-all | bytes 16384 | tf_op jit(solution)/shard_map/all_to_all | solution.py:188
  253.8 4.5 all-to-all-start.4
  259.8 6.2 gather_fusion
  267.0 6.2 gather_fusion.1
  273.7 4.5 scatter_custom_fusion.3
  279.6 7.5 %all-to-all-start.5 = ((f32[32,32,2]{0,2,1:T(2,128)}), f32[32,32,2]{0,2,1:T(2,128)S(1)}, u32[]{:S(2)}, u32[]{:S(2)}) async-start(f32[32,32,2]{0,2,1:T(2,128)} %copy.148), calls=%async_computation.5 | async-start | bytes 65536 | tf_op jit(solution)/shard_map/all_to_all | solution.py:217
  294.4 6.2 all-to-all-start.3
  302.1 5.8 all-to-all-done.3
  308.1 212.7 %while.28 = (s32[]{:T(128)}, f32[4,8,64,768]{3,1,0,2:T(8,128)}, f32[4,16,96,8]{1,3,2,0:T(8,128)}, s32[4,8,64,9]{2,1,3,0:T(8,128)S(1)}, f32[4,8,64,1024]{3,2,1,0:...) while((s32[]{:T(128)}, f32[4,8,64,768]{3,1,0,2:T(8,128)}, ...), condition=%wide.region_15.16_spmd.clone, body=%wide.region_13.15_spmd.clone.sunk | while | flops 1788871168 | bytes 67385192 | solution.py:129
  309.1 7.1 %select_reduce_fusion.2 = f32[8,64,1024]{2,1,0:T(8,128)} fusion(f32[8]{0:T(128)S(1)} %subtract_multiply_fusion.2, s32[8,64,8]{2,1,0:T(8,128)S(1)} %copy.187), kind=kLoop, calls=%fused_computation.21.clone.1 | loop fusion | flops 12058624 | bytes 2113568 | tf_op jit(solution)/shard_map/while/body/eval_jaxpr/reduce_sum | solution.py:112
  320.4 9.3 %bitcast_compare_fusion.5 = pred[8,1536,1024]{2,1,0:T(32,128)(4,1)} fusion(s32[1536]{0:T(1024)S(1)} %eq.184, s32[8,96,1024]{2,1,0:T(8,128)S(1)} %dynamic-slice_bitcast_fusion.15), kind=kLoop, calls=%fused_computation.19.clone.1 | loop fusion | flops 12582912 | bytes 15734784 | tf_op jit(solution)/shard_map/while/body/eval_jaxpr/eq | solution.py:54
  329.7 12.8 %fusion.84 = f32[8,64,1536]{1,2,0:T(8,128)} fusion(pred[8,1536,1024]{2,1,0:T(32,128)(4,1)} %bitcast_compare_fusion.5, f32[8,64,1024]{2,1,0:T(8,128)} %select_reduce_fusion.2, f32[4,8,64,1024]{3,2,1,0:T(8,128)} %get-tuple-element.426, s32[]{:T(128)} %get-tuple-element.411, f32[8,64]{1,0:T(8,128)S(1)} %get-tuple-element.371, ...), kind=kOutput, calls=%fused_computation.38.clone.1 | convolution fusion | flops 1613234176 | bytes 19928576 | tf_op jit(solution)/shard_map/while/body/eval_jaxpr/grl,gkl->grk/dot_general | solution.py:118
  342.6 5.5 fusion.85
  353.1 8.3 %fusion.86 = f32[4,16,96,8]{1,3,2,0:T(8,128)} fusion(f32[4,16,96,8]{1,3,2,0:T(8,128)} %get-tuple-element.413, s32[]{:T(128)} %get-tuple-element.411, f32[8,64,96,16]{1,3,2,0:T(8,128)} %bitcast.164, bf16[4,8,64,768]{2,3,1,0:T(8,128)(2,1)} %get-tuple-element.431), kind=kOutput, calls=%fused_computation.37.clone.1 | convolution fusion | flops 75497472 | bytes 8258560 | tf_op jit(solution)/shard_map/while/body/eval_jaxpr/grmk,grme->kme/dot_general | solution.py:126
  362.2 7.1 %select_reduce_fusion.2 = f32[8,64,1024]{2,1,0:T(8,128)} fusion(f32[8]{0:T(128)S(1)} %subtract_multiply_fusion.2, s32[8,64,8]{2,1,0:T(8,128)S(1)} %copy.187), kind=kLoop, calls=%fused_computation.21.clone.1 | loop fusion | flops 12058624 | bytes 2113568 | tf_op jit(solution)/shard_map/while/body/eval_jaxpr/reduce_sum | solution.py:112
  373.5 9.3 %bitcast_compare_fusion.5 = pred[8,1536,1024]{2,1,0:T(32,128)(4,1)} fusion(s32[1536]{0:T(1024)S(1)} %eq.184, s32[8,96,1024]{2,1,0:T(8,128)S(1)} %dynamic-slice_bitcast_fusion.15), kind=kLoop, calls=%fused_computation.19.clone.1 | loop fusion | flops 12582912 | bytes 15734784 | tf_op jit(solution)/shard_map/while/body/eval_jaxpr/eq | solution.py:54
  382.8 12.8 %fusion.84 = f32[8,64,1536]{1,2,0:T(8,128)} fusion(pred[8,1536,1024]{2,1,0:T(32,128)(4,1)} %bitcast_compare_fusion.5, f32[8,64,1024]{2,1,0:T(8,128)} %select_reduce_fusion.2, f32[4,8,64,1024]{3,2,1,0:T(8,128)} %get-tuple-element.426, s32[]{:T(128)} %get-tuple-element.411, f32[8,64]{1,0:T(8,128)S(1)} %get-tuple-element.371, ...), kind=kOutput, calls=%fused_computation.38.clone.1 | convolution fusion | flops 1613234176 | bytes 19928576 | tf_op jit(solution)/shard_map/while/body/eval_jaxpr/grl,gkl->grk/dot_general | solution.py:118
  395.6 5.5 fusion.85
  406.2 8.2 %fusion.86 = f32[4,16,96,8]{1,3,2,0:T(8,128)} fusion(f32[4,16,96,8]{1,3,2,0:T(8,128)} %get-tuple-element.413, s32[]{:T(128)} %get-tuple-element.411, f32[8,64,96,16]{1,3,2,0:T(8,128)} %bitcast.164, bf16[4,8,64,768]{2,3,1,0:T(8,128)(2,1)} %get-tuple-element.431), kind=kOutput, calls=%fused_computation.37.clone.1 | convolution fusion | flops 75497472 | bytes 8258560 | tf_op jit(solution)/shard_map/while/body/eval_jaxpr/grmk,grme->kme/dot_general | solution.py:126
  415.2 7.1 %select_reduce_fusion.2 = f32[8,64,1024]{2,1,0:T(8,128)} fusion(f32[8]{0:T(128)S(1)} %subtract_multiply_fusion.2, s32[8,64,8]{2,1,0:T(8,128)S(1)} %copy.187), kind=kLoop, calls=%fused_computation.21.clone.1 | loop fusion | flops 12058624 | bytes 2113568 | tf_op jit(solution)/shard_map/while/body/eval_jaxpr/reduce_sum | solution.py:112
  426.5 9.3 %bitcast_compare_fusion.5 = pred[8,1536,1024]{2,1,0:T(32,128)(4,1)} fusion(s32[1536]{0:T(1024)S(1)} %eq.184, s32[8,96,1024]{2,1,0:T(8,128)S(1)} %dynamic-slice_bitcast_fusion.15), kind=kLoop, calls=%fused_computation.19.clone.1 | loop fusion | flops 12582912 | bytes 15734784 | tf_op jit(solution)/shard_map/while/body/eval_jaxpr/eq | solution.py:54
  435.9 12.8 %fusion.84 = f32[8,64,1536]{1,2,0:T(8,128)} fusion(pred[8,1536,1024]{2,1,0:T(32,128)(4,1)} %bitcast_compare_fusion.5, f32[8,64,1024]{2,1,0:T(8,128)} %select_reduce_fusion.2, f32[4,8,64,1024]{3,2,1,0:T(8,128)} %get-tuple-element.426, s32[]{:T(128)} %get-tuple-element.411, f32[8,64]{1,0:T(8,128)S(1)} %get-tuple-element.371, ...), kind=kOutput, calls=%fused_computation.38.clone.1 | convolution fusion | flops 1613234176 | bytes 19928576 | tf_op jit(solution)/shard_map/while/body/eval_jaxpr/grl,gkl->grk/dot_general | solution.py:118
  448.7 5.5 fusion.85
  459.3 8.2 %fusion.86 = f32[4,16,96,8]{1,3,2,0:T(8,128)} fusion(f32[4,16,96,8]{1,3,2,0:T(8,128)} %get-tuple-element.413, s32[]{:T(128)} %get-tuple-element.411, f32[8,64,96,16]{1,3,2,0:T(8,128)} %bitcast.164, bf16[4,8,64,768]{2,3,1,0:T(8,128)(2,1)} %get-tuple-element.431), kind=kOutput, calls=%fused_computation.37.clone.1 | convolution fusion | flops 75497472 | bytes 8258560 | tf_op jit(solution)/shard_map/while/body/eval_jaxpr/grmk,grme->kme/dot_general | solution.py:126
  468.3 7.1 %select_reduce_fusion.2 = f32[8,64,1024]{2,1,0:T(8,128)} fusion(f32[8]{0:T(128)S(1)} %subtract_multiply_fusion.2, s32[8,64,8]{2,1,0:T(8,128)S(1)} %copy.187), kind=kLoop, calls=%fused_computation.21.clone.1 | loop fusion | flops 12058624 | bytes 2113568 | tf_op jit(solution)/shard_map/while/body/eval_jaxpr/reduce_sum | solution.py:112
  479.6 9.3 %bitcast_compare_fusion.5 = pred[8,1536,1024]{2,1,0:T(32,128)(4,1)} fusion(s32[1536]{0:T(1024)S(1)} %eq.184, s32[8,96,1024]{2,1,0:T(8,128)S(1)} %dynamic-slice_bitcast_fusion.15), kind=kLoop, calls=%fused_computation.19.clone.1 | loop fusion | flops 12582912 | bytes 15734784 | tf_op jit(solution)/shard_map/while/body/eval_jaxpr/eq | solution.py:54
  489.0 12.8 %fusion.84 = f32[8,64,1536]{1,2,0:T(8,128)} fusion(pred[8,1536,1024]{2,1,0:T(32,128)(4,1)} %bitcast_compare_fusion.5, f32[8,64,1024]{2,1,0:T(8,128)} %select_reduce_fusion.2, f32[4,8,64,1024]{3,2,1,0:T(8,128)} %get-tuple-element.426, s32[]{:T(128)} %get-tuple-element.411, f32[8,64]{1,0:T(8,128)S(1)} %get-tuple-element.371, ...), kind=kOutput, calls=%fused_computation.38.clone.1 | convolution fusion | flops 1613234176 | bytes 19928576 | tf_op jit(solution)/shard_map/while/body/eval_jaxpr/grl,gkl->grk/dot_general | solution.py:118
  501.8 5.5 fusion.85
  512.4 8.2 %fusion.86 = f32[4,16,96,8]{1,3,2,0:T(8,128)} fusion(f32[4,16,96,8]{1,3,2,0:T(8,128)} %get-tuple-element.413, s32[]{:T(128)} %get-tuple-element.411, f32[8,64,96,16]{1,3,2,0:T(8,128)} %bitcast.164, bf16[4,8,64,768]{2,3,1,0:T(8,128)(2,1)} %get-tuple-element.431), kind=kOutput, calls=%fused_computation.37.clone.1 | convolution fusion | flops 75497472 | bytes 8258560 | tf_op jit(solution)/shard_map/while/body/eval_jaxpr/grmk,grme->kme/dot_general | solution.py:126
  523.2 84.9 %all_to_all.36 = f32[32,32,2,768]{3,0,2,1:T(8,128)S(1)} all-to-all(f32[32,32,2,768]{3,0,2,1:T(8,128)} %bitcast.170), channel_id=1, replica_groups=mesh['corpus'=32,'query'=4] {'corpus'}, dimensions={1} | all-to-all | bytes 12582912 | tf_op jit(solution)/shard_map/all_to_all | solution.py:232
  608.0 7.5 %copy.154 = f32[32,32,2,768]{3,2,1,0:T(2,128)} copy(f32[32,32,2,768]{3,0,2,1:T(8,128)S(1)} %all_to_all.36) | data formatting | bytes 12582912 | tf_op jit(solution)/shard_map/all_to_all | solution.py:232
  615.5 8.5 %reshape.318 = f32[2048,768]{1,0:T(8,128)} reshape(f32[32,32,2,768]{3,2,1,0:T(2,128)} %copy.154) | data formatting | bytes 12582912 | tf_op jit(solution)/shard_map/reshape | solution.py:239
  624.0 8.7 %gather_fusion.2 = f32[1024,768]{1,0:T(8,128)} fusion(f32[2048,768]{1,0:T(8,128)} %reshape.318, s32[1024]{0:T(1024)S(1)} %copy-done.13), kind=kCustom, calls=%fused_computation.2 | custom fusion | bytes 6295552 | tf_op jit(solution)/shard_map/gather | solution.py:239
  (243 shorter events, 146.8 us)
Async XLA Ops:
  8.9 1.9 copy-start.1
  16.0 0.8 copy-start.15
  16.8 16.1 %copy-start.6 = (bf16[256,768]{1,0:T(8,128)(2,1)S(1)}, bf16[256,768]{1,0:T(8,128)(2,1)}, u32[]{:S(2)}) copy-start(bf16[256,768]{1,0:T(8,128)(2,1)} %param.9) | copy-start | bytes 1179652
  17.5 17.1 %copy-start.14 = (s32[1024,1]{0,1:T(1,128)}, s32[1024,1]{0,1:T(1,128)S(1)}, u32[]{:S(2)}) copy-start(s32[1024,1]{0,1:T(1,128)S(1)} %compare_select_fusion.1) | copy-start | bytes 12292
  23.2 28.0 %all-to-all-start = ((s32[32,1,576]{2,1,0:T(1,128)}), s32[32,1,576]{2,1,0:T(1,128)S(1)}, u32[]{:S(2)}, u32[]{:S(2)}) async-start(s32[32,1,576]{2,1,0:T(1,128)} %reshape.389), calls=%async_computation | async-start | bytes 163840 | tf_op jit(solution)/shard_map/all_to_all | solution.py:173
  51.2 7.8 %copy-start.7 = (s32[32,1,576]{2,1,0:T(1,128)}, s32[32,1,576]{2,1,0:T(1,128)S(1)}, u32[]{:S(2)}) copy-start(s32[32,1,576]{2,1,0:T(1,128)S(1)} %all-to-all-done) | copy-start | bytes 221188
  51.2 47.3 %all-to-all-start.1 = ((bf16[32,32,2,768]{3,2,0,1:T(2,128)(2,1)}), bf16[32,32,2,768]{3,2,0,1:T(2,128)(2,1)S(1)}, u32[]{:S(2)}, u32[]{:S(2)}) async-start(bf16[32,32,2,768]{3,2,0,1:T(2,128)(2,1)} %copy.136), calls=%async_computation.1 | async-start | bytes 6291456 | tf_op jit(solution)/shard_map/all_to_all | solution.py:166
  65.7 0.7 copy-start.2
  119.5 9.4 %copy-start = (bf16[8,64,96,16]{1,3,2,0:T(8,128)(2,1)S(1)}, bf16[8,64,96,16]{1,3,2,0:T(8,128)(2,1)}, u32[]{:S(2)}) copy-start(bf16[8,64,96,16]{1,3,2,0:T(8,128)(2,1)} %copy.185) | copy-start | bytes 4718596 | tf_op jit(solution)/shard_map/while
  151.9 9.4 %copy-start = (bf16[8,64,96,16]{1,3,2,0:T(8,128)(2,1)S(1)}, bf16[8,64,96,16]{1,3,2,0:T(8,128)(2,1)}, u32[]{:S(2)}) copy-start(bf16[8,64,96,16]{1,3,2,0:T(8,128)(2,1)} %copy.185) | copy-start | bytes 4718596 | tf_op jit(solution)/shard_map/while
  184.3 9.4 %copy-start = (bf16[8,64,96,16]{1,3,2,0:T(8,128)(2,1)S(1)}, bf16[8,64,96,16]{1,3,2,0:T(8,128)(2,1)}, u32[]{:S(2)}) copy-start(bf16[8,64,96,16]{1,3,2,0:T(8,128)(2,1)} %copy.185) | copy-start | bytes 4718596 | tf_op jit(solution)/shard_map/while
  216.7 9.4 %copy-start = (bf16[8,64,96,16]{1,3,2,0:T(8,128)(2,1)S(1)}, bf16[8,64,96,16]{1,3,2,0:T(8,128)(2,1)}, u32[]{:S(2)}) copy-start(bf16[8,64,96,16]{1,3,2,0:T(8,128)(2,1)} %copy.185) | copy-start | bytes 4718596 | tf_op jit(solution)/shard_map/while
  253.8 12.4 %all-to-all-start.4 = ((f32[32,32,2]{0,2,1:T(2,128)}), f32[32,32,2]{0,2,1:T(2,128)S(1)}, u32[]{:S(2)}, u32[]{:S(2)}) async-start(f32[32,32,2]{0,2,1:T(2,128)} %get-tuple-element.251), calls=%async_computation.4 | async-start | bytes 65536 | tf_op jit(solution)/shard_map/all_to_all | solution.py:195
  259.0 14.2 %copy-start.12 = (s32[1024]{0:T(1024)}, s32[1024]{0:T(1024)S(1)}, u32[]{:S(2)}) copy-start(s32[1024]{0:T(1024)S(1)} %broadcast_clamp_fusion) | copy-start | bytes 12292
  266.2 34.6 %copy-start.3 = (s32[32,32,2,9]{0,2,1,3:T(2,128)S(1)}, s32[32,32,2,9]{0,2,1,3:T(2,128)}, u32[]{:S(2)}) copy-start(s32[32,32,2,9]{0,2,1,3:T(2,128)} %copy-done.2) | copy-start | bytes 221188
  279.6 14.8 %all-to-all-start.5 = ((f32[32,32,2]{0,2,1:T(2,128)}), f32[32,32,2]{0,2,1:T(2,128)S(1)}, u32[]{:S(2)}, u32[]{:S(2)}) async-start(f32[32,32,2]{0,2,1:T(2,128)} %copy.148), calls=%async_computation.5 | async-start | bytes 65536 | tf_op jit(solution)/shard_map/all_to_all | solution.py:217
  294.4 13.5 %all-to-all-start.3 = ((f32[32,32,2]{0,2,1:T(2,128)}), f32[32,32,2]{0,2,1:T(2,128)S(1)}, u32[]{:S(2)}, u32[]{:S(2)}) async-start(f32[32,32,2]{0,2,1:T(2,128)} %copy.144), calls=%async_computation.3 | async-start | bytes 65536 | tf_op jit(solution)/shard_map/all_to_all | solution.py:210
  300.6 338.0 %all-gather.2.cloned.1.call-start = ((), (), s32[]{:S(2)}) async-start(), calls=%async_computation.7 | async-start | bytes 6340608 | tf_op jit(solution)/shard_map/all_gather | solution.py:241
  308.3 0.6 copy-start.8
  308.3 0.6 copy-start.10
  308.3 8.5 %copy-start.4 = (s32[4,8,64,9]{2,1,3,0:T(8,128)}, s32[4,8,64,9]{2,1,3,0:T(8,128)S(1)}, u32[]{:S(2)}) copy-start(s32[4,8,64,9]{2,1,3,0:T(8,128)S(1)} %get-tuple-element.425) | copy-start | bytes 221188 | tf_op jit(solution)/shard_map/while
  353.1 8.3 %copy-start.5 = (s32[4,8,64,9]{2,1,3,0:T(8,128)S(1)}, s32[4,8,64,9]{2,1,3,0:T(8,128)}, u32[]{:S(2)}) copy-start(s32[4,8,64,9]{2,1,3,0:T(8,128)} %copy-done.4) | copy-start | bytes 221188 | tf_op jit(solution)/shard_map/while
  353.1 8.3 %copy-start.9 = (f32[4,8,64]{2,1,0:T(8,128)S(1)}, f32[4,8,64]{2,1,0:T(8,128)}, u32[]{:S(2)}) copy-start(f32[4,8,64]{2,1,0:T(8,128)} %copy-done.8) | copy-start | bytes 24580 | tf_op jit(solution)/shard_map/while
  353.1 8.3 %copy-start.11 = (f32[4,8,64]{2,1,0:T(8,128)S(1)}, f32[4,8,64]{2,1,0:T(8,128)}, u32[]{:S(2)}) copy-start(f32[4,8,64]{2,1,0:T(8,128)} %copy-done.10) | copy-start | bytes 24580 | tf_op jit(solution)/shard_map/while
  361.4 0.6 copy-start.8
  361.4 0.6 copy-start.10
  361.4 8.5 %copy-start.4 = (s32[4,8,64,9]{2,1,3,0:T(8,128)}, s32[4,8,64,9]{2,1,3,0:T(8,128)S(1)}, u32[]{:S(2)}) copy-start(s32[4,8,64,9]{2,1,3,0:T(8,128)S(1)} %get-tuple-element.425) | copy-start | bytes 221188 | tf_op jit(solution)/shard_map/while
  406.2 8.2 %copy-start.5 = (s32[4,8,64,9]{2,1,3,0:T(8,128)S(1)}, s32[4,8,64,9]{2,1,3,0:T(8,128)}, u32[]{:S(2)}) copy-start(s32[4,8,64,9]{2,1,3,0:T(8,128)} %copy-done.4) | copy-start | bytes 221188 | tf_op jit(solution)/shard_map/while
  406.2 8.2 %copy-start.9 = (f32[4,8,64]{2,1,0:T(8,128)S(1)}, f32[4,8,64]{2,1,0:T(8,128)}, u32[]{:S(2)}) copy-start(f32[4,8,64]{2,1,0:T(8,128)} %copy-done.8) | copy-start | bytes 24580 | tf_op jit(solution)/shard_map/while
  406.2 8.2 %copy-start.11 = (f32[4,8,64]{2,1,0:T(8,128)S(1)}, f32[4,8,64]{2,1,0:T(8,128)}, u32[]{:S(2)}) copy-start(f32[4,8,64]{2,1,0:T(8,128)} %copy-done.10) | copy-start | bytes 24580 | tf_op jit(solution)/shard_map/while
  414.4 0.6 copy-start.8
  414.5 0.6 copy-start.10
  414.5 8.5 %copy-start.4 = (s32[4,8,64,9]{2,1,3,0:T(8,128)}, s32[4,8,64,9]{2,1,3,0:T(8,128)S(1)}, u32[]{:S(2)}) copy-start(s32[4,8,64,9]{2,1,3,0:T(8,128)S(1)} %get-tuple-element.425) | copy-start | bytes 221188 | tf_op jit(solution)/shard_map/while
  459.3 8.3 %copy-start.5 = (s32[4,8,64,9]{2,1,3,0:T(8,128)S(1)}, s32[4,8,64,9]{2,1,3,0:T(8,128)}, u32[]{:S(2)}) copy-start(s32[4,8,64,9]{2,1,3,0:T(8,128)} %copy-done.4) | copy-start | bytes 221188 | tf_op jit(solution)/shard_map/while
  459.3 8.3 %copy-start.9 = (f32[4,8,64]{2,1,0:T(8,128)S(1)}, f32[4,8,64]{2,1,0:T(8,128)}, u32[]{:S(2)}) copy-start(f32[4,8,64]{2,1,0:T(8,128)} %copy-done.8) | copy-start | bytes 24580 | tf_op jit(solution)/shard_map/while
  459.3 8.3 %copy-start.11 = (f32[4,8,64]{2,1,0:T(8,128)S(1)}, f32[4,8,64]{2,1,0:T(8,128)}, u32[]{:S(2)}) copy-start(f32[4,8,64]{2,1,0:T(8,128)} %copy-done.10) | copy-start | bytes 24580 | tf_op jit(solution)/shard_map/while
  467.5 0.6 copy-start.8
  467.5 0.6 copy-start.10
  467.5 8.5 %copy-start.4 = (s32[4,8,64,9]{2,1,3,0:T(8,128)}, s32[4,8,64,9]{2,1,3,0:T(8,128)S(1)}, u32[]{:S(2)}) copy-start(s32[4,8,64,9]{2,1,3,0:T(8,128)S(1)} %get-tuple-element.425) | copy-start | bytes 221188 | tf_op jit(solution)/shard_map/while
  512.4 8.2 %copy-start.5 = (s32[4,8,64,9]{2,1,3,0:T(8,128)S(1)}, s32[4,8,64,9]{2,1,3,0:T(8,128)}, u32[]{:S(2)}) copy-start(s32[4,8,64,9]{2,1,3,0:T(8,128)} %copy-done.4) | copy-start | bytes 221188 | tf_op jit(solution)/shard_map/while
  512.4 8.2 %copy-start.9 = (f32[4,8,64]{2,1,0:T(8,128)S(1)}, f32[4,8,64]{2,1,0:T(8,128)}, u32[]{:S(2)}) copy-start(f32[4,8,64]{2,1,0:T(8,128)} %copy-done.8) | copy-start | bytes 24580 | tf_op jit(solution)/shard_map/while
  512.4 8.2 %copy-start.11 = (f32[4,8,64]{2,1,0:T(8,128)S(1)}, f32[4,8,64]{2,1,0:T(8,128)}, u32[]{:S(2)}) copy-start(f32[4,8,64]{2,1,0:T(8,128)} %copy-done.10) | copy-start | bytes 24580 | tf_op jit(solution)/shard_map/while
  615.5 8.5 %copy-start.13 = (s32[1024]{0:T(1024)S(1)}, s32[1024]{0:T(1024)}, u32[]{:S(2)}) copy-start(s32[1024]{0:T(1024)} %copy-done.12) | copy-start | bytes 12292
Sparse Core Ops, SparseCore 0:
  523.3 90.4 all-gather.1
